TPU v7x, 32 devices: a whole 2x2x4 slice. The times are simulated.
32 devices in a mesh: seq: 8 (over z, y), head: 4 (over x, core).
Axes of the slice: x: 2, y: 2, z: 4, core: 2. Of those that a mesh axis runs over, the one named last changes fastest.
Arguments:
- tokens: bfloat16 [2048, 1024], P('seq'), may hold values from -6 to 6
- w_qkv: bfloat16 [1024, 3, 1024], P('seq', None, 'head'), may hold values from -0.1875 to 0.1875
- w_out: bfloat16 [1024, 1024], P('head', 'seq'), may hold values from -1 to 1
- ln1_gain: bfloat16 [1024], P('seq'), may hold values from 0.5 to 1.5
- ln1_bias: bfloat16 [1024], P('seq'), may hold values from -1.796875 to 1.796875
- ln2_gain: bfloat16 [1024], P('seq'), may hold values from 0.5 to 1.5
- ln2_bias: bfloat16 [1024], P('seq'), may hold values from -1.796875 to 1.796875
- w_up: bfloat16 [1024, 4096], P('seq', 'head'), may hold values from -0.1875 to 0.1875
- up_bias: bfloat16 [4096], P('head'), may hold values from -1.796875 to 1.796875
- w_down: bfloat16 [4096, 1024], P('head', 'seq'), may hold values from -0.09375 to 0.09375
- down_bias: bfloat16 [1024], P('seq'), may hold values from -1.796875 to 1.796875
- seq_units: int32 [4], replicated, may hold values from 1 to 4, 8 in all
- seq_pad: int32 [4], replicated, may hold values from 0 to 127
- rand_picks: int32 [32, 16, 3], P('seq', 'head'), may hold values from 0 to 65535
- cotangent: bfloat16 [2048, 1024], P('seq'), may hold values from -6 to 6
Outputs:
- output: bfloat16 [2048, 1024], P('seq')
- x_grad: float32 [2048, 1024], P('seq')
- w_qkv_grad: float32 [1024, 3, 1024], P('seq', None, 'head')
- w_out_grad: float32 [1024, 1024], P('head', 'seq')
- ln1_gain_grad: float32 [1024], P('seq')
- ln1_bias_grad: float32 [1024], P('seq')
- ln2_gain_grad: float32 [1024], P('seq')
- ln2_bias_grad: float32 [1024], P('seq')
- w_up_grad: float32 [1024, 4096], P('seq', 'head')
- up_bias_grad: float32 [4096], P('head')
- w_down_grad: float32 [4096, 1024], P('head', 'seq')
- down_bias_grad: float32 [1024], P('seq')
Inputs may be any that keep to these rules, and one draw needn't show every extreme that they name: `seq_units`: each sequence covers whole units; the values add up to the number of units in the stream, and some sequence covers 4 units.
All inputs are finite; a program needn't handle non-finite values.
Results may differ from a plain program's by a relative error of at most 0.012.
Values may be sent and summed in bfloat16 or wider, within the bound.
A program may use at most 128 MiB of HBM per device.

v0:
```python
import jax
import jax.numpy as jnp
from jax import lax
from jax.sharding import PartitionSpec as P

HEAD_DIM = 64
BLK = 64
SPAN = 4
BLK_DEV = 4
EPSILON = 1e-05
NEGATIVE = -1e30
F32 = jnp.float32
BF16 = jnp.bfloat16


def shifted(value, axis, steps):
    count = lax.axis_size(axis)
    first, last = (max(0, -steps), min(count, count - steps))
    return lax.ppermute(value, axis, [(i, i + steps) for i in range(first, last)])


def norm_parts(features):
    average = jnp.mean(features, axis=-1, keepdims=True)
    centred = features - average
    spread = jnp.mean(centred * centred, axis=-1, keepdims=True)
    inverse = lax.rsqrt(spread + EPSILON)
    return (centred * inverse, inverse)


def norm_backward(xhat, inverse, scaled):
    first = jnp.mean(scaled, axis=-1, keepdims=True)
    second = jnp.mean(scaled * xhat, axis=-1, keepdims=True)
    return inverse * (scaled - first - xhat * second)


def dot(a, b, dims):
    return lax.dot_general(a, b, (dims, ((), ())), preferred_element_type=F32)


def sequence_place(seq_units, seq_pad):
    device = lax.axis_index("seq")
    start, leader, span, pad = (0, 0, 0, 0)
    for k in range(seq_units.shape[0]):
        units = seq_units[k]
        inside = (device >= start) & (device < start + units)
        leader = jnp.where(inside, start, leader)
        span = jnp.where(inside, units, span)
        pad = jnp.where(inside, seq_pad[k], pad)
        start = start + units
    return (device - leader, span, pad)


def key_counts(position, span, picks):
    blocks = lax.broadcasted_iota(jnp.int32, (1, 1, SPAN * BLK_DEV), 2)
    query = position * BLK_DEV + lax.broadcasted_iota(jnp.int32, (BLK_DEV, 1, 1), 0)
    total = span * BLK_DEV
    count = jnp.zeros((BLK_DEV, picks.shape[1], SPAN * BLK_DEV), F32)
    for wanted in (query - 1, query, query + 1, 0, total - 1):
        count = count + (blocks == wanted).astype(F32)
    chosen = picks % total
    for r in range(picks.shape[2]):
        count = count + (blocks == chosen[:, :, r : r + 1]).astype(F32)
    return jnp.where((query == 0) | (query == total - 1), 1.0, count)


def local_general(
    tokens,
    w_qkv,
    w_out,
    ln1_gain,
    ln1_bias,
    ln2_gain,
    ln2_bias,
    w_up,
    up_bias,
    w_down,
    down_bias,
    seq_units,
    seq_pad,
    rand_picks,
    cotangent,
):
    tok, width = tokens.shape
    heads = w_qkv.shape[2] // HEAD_DIM
    rows = lambda v: lax.all_gather(v, "seq", axis=0, tiled=True)
    cols = lambda v: lax.all_gather(v, "seq", axis=1, tiled=True)
    vectors = jnp.stack([ln1_gain, ln1_bias, ln2_gain, ln2_bias, down_bias], axis=0)
    gain_one, shift_one, gain_two, shift_two, down_shift = [
        v[None].astype(F32) for v in cols(vectors)
    ]
    qkv = rows(w_qkv)
    out_w, up_w, down_w = (cols(w_out), rows(w_up), cols(w_down))
    position, span, pad = sequence_place(seq_units, seq_pad)
    root = SPAN - 1 - position
    inputs = tokens.astype(F32)
    xhat_one, inv_one = norm_parts(inputs)
    normed = (xhat_one * gain_one + shift_one).astype(BF16)
    triple = jnp.einsum("td,dcf->tcf", normed, qkv, preferred_element_type=F32).astype(BF16)
    own = jnp.stack([triple[:, 1], triple[:, 2]], axis=0)
    pieces = [own if o == 0 else shifted(own, "seq", -o) for o in range(1 - SPAN, SPAN)]
    nearby = jnp.stack(pieces, axis=0)
    window = lax.dynamic_slice_in_dim(nearby, root, SPAN, 0)
    split = lambda v: v.reshape(v.shape[0], heads, HEAD_DIM)
    keys = split(window[:, 0].reshape(SPAN * tok, -1))
    values = split(window[:, 1].reshape(SPAN * tok, -1))
    queries = split(triple[:, 0])
    scaling = HEAD_DIM ** (-0.5)
    live = jnp.arange(SPAN * tok, dtype=jnp.int32) < span * tok - pad
    count = jnp.repeat(key_counts(position, span, rand_picks), BLK, axis=2)
    count = jnp.where(live[None, None], count, 0.0)
    count = jnp.transpose(jnp.repeat(count, BLK, axis=0), (1, 0, 2))
    logits = jnp.einsum("qhd,khd->hqk", queries, keys, preferred_element_type=F32) * scaling
    logits = jnp.where(count > 0, logits, NEGATIVE)
    grown = jnp.exp(logits - jnp.max(logits, axis=-1, keepdims=True)) * count
    chances = grown / jnp.sum(grown, axis=-1, keepdims=True)
    chances_low = chances.astype(BF16)
    attended = jnp.einsum("hqk,khd->qhd", chances_low, values, preferred_element_type=F32)
    attended = attended.astype(BF16).reshape(tok, heads * HEAD_DIM)
    middle = inputs + lax.psum(dot(attended, out_w, ((1,), (0,))), "head")
    xhat_two, inv_two = norm_parts(middle)
    normed_two = (xhat_two * gain_two + shift_two).astype(BF16)
    pre_act = dot(normed_two, up_w, ((1,), (0,))) + up_bias.astype(F32)[None]
    hidden, pull = jax.vjp(lambda v: jax.nn.gelu(v, approximate=True), pre_act)
    hidden = hidden.astype(BF16)
    ffn = lax.psum(dot(hidden, down_w, ((1,), (0,))).astype(BF16), "head").astype(F32)
    output = (middle + ffn + down_shift).astype(BF16)
    grad_out = cotangent.astype(F32)
    grad_w_down = dot(hidden, cotangent, ((0,), (0,)))
    grad_pre = pull(dot(cotangent, down_w, ((1,), (1,))))[0].astype(BF16)
    grad_w_up = dot(normed_two, grad_pre, ((0,), (0,)))
    grad_up_bias = lax.psum(jnp.sum(grad_pre.astype(F32), axis=0), "seq")
    grad_two = lax.psum(dot(grad_pre, up_w, ((1,), (1,))), "head")
    grad_middle = grad_out + norm_backward(xhat_two, inv_two, grad_two * gain_two)
    grad_branch = grad_middle.astype(BF16)
    grad_w_out = dot(attended, grad_branch, ((0,), (0,)))
    grad_att = split(dot(grad_branch, out_w, ((1,), (1,))).astype(BF16))
    grad_prob = jnp.einsum("qhd,khd->hqk", grad_att, values, preferred_element_type=F32)
    inner = jnp.sum(chances * grad_prob, axis=-1, keepdims=True)
    grad_logit = (chances * (grad_prob - inner)).astype(BF16)
    dq = scaling * jnp.einsum("hqk,khd->qhd", grad_logit, keys, preferred_element_type=F32)
    dk = scaling * jnp.einsum("hqk,qhd->khd", grad_logit, queries, preferred_element_type=F32)
    dv = jnp.einsum("hqk,qhd->khd", chances_low, grad_att, preferred_element_type=F32)
    part = jnp.stack([dk.reshape(SPAN, tok, -1), dv.reshape(SPAN, tok, -1)], axis=1)
    near = jnp.zeros((2 * SPAN - 1,) + part.shape[1:], F32)
    near = lax.dynamic_update_slice_in_dim(near, part, root, 0)
    owned = near[SPAN - 1]
    for offset in range(1 - SPAN, SPAN):
        if offset:
            owned = owned + shifted(near[offset + SPAN - 1], "seq", offset)
    owned = owned.astype(BF16)
    grad_triple = jnp.stack([dq.reshape(tok, -1).astype(BF16), owned[0], owned[1]], axis=1)
    grad_w_qkv = jnp.einsum("td,tcf->dcf", normed, grad_triple, preferred_element_type=F32)
    grad_one = lax.psum(
        jnp.einsum("tcf,dcf->td", grad_triple, qkv, preferred_element_type=F32), "head"
    )
    x_grad = grad_middle + norm_backward(xhat_one, inv_one, grad_one * gain_one)
    sums = jnp.stack(
        [
            jnp.sum(grad_one * xhat_one, axis=0),
            jnp.sum(grad_one, axis=0),
            jnp.sum(grad_two * xhat_two, axis=0),
            jnp.sum(grad_two, axis=0),
            jnp.sum(grad_out, axis=0),
        ],
        axis=0,
    )
    scatter = lambda v, d: lax.psum_scatter(v, "seq", scatter_dimension=d, tiled=True)
    sums = scatter(sums, 1)
    return (
        output,
        x_grad,
        scatter(grad_w_qkv, 0),
        scatter(grad_w_out, 1),
        sums[0],
        sums[1],
        sums[2],
        sums[3],
        scatter(grad_w_up, 0),
        grad_up_bias,
        scatter(grad_w_down, 1),
        sums[4],
    )


IN_SPECS = (
    P("seq", None),
    P("seq", None, "head"),
    P("head", "seq"),
    P("seq"),
    P("seq"),
    P("seq"),
    P("seq"),
    P("seq", "head"),
    P("head"),
    P("head", "seq"),
    P("seq"),
    P(),
    P(),
    P("seq", "head", None),
    P("seq", None),
)
OUT_SPECS = (
    P("seq", None),
    P("seq", None),
    P("seq", None, "head"),
    P("head", "seq"),
    P("seq"),
    P("seq"),
    P("seq"),
    P("seq"),
    P("seq", "head"),
    P("head"),
    P("head", "seq"),
    P("seq"),
)


def solution(mesh):
    return jax.shard_map(
        local_general, mesh=mesh, in_specs=IN_SPECS, out_specs=OUT_SPECS, check_vma=False
    )
```

profile of v0, /device:TPU:0, one launch (start us, length us, event | category | flops | bytes accessed | tf_op | source)
XLA Modules:
  0.0 851.5 jit_solution(9352380124314227854)
XLA Ops:
  23.5 27.9 %all_gather.15 = bf16[5,1024]{1,0:T(8,128)(2,1)S(1)} all-gather(bf16[5,128]{1,0:T(8,128)(2,1)S(1)} %stack.75), channel_id=1, replica_groups=mesh['seq'=8,'head'=4] {'seq'}, dimensions={1}, use_global_device_ids=true | all-gather | bytes 11520 | tf_op jit(solution)/shard_map/all_gather | solution.py:86
  54.2 27.8 %all_gather.17 = bf16[256,1024]{1,0:T(8,128)(2,1)S(1)} all-gather(bf16[256,128]{1,0:T(8,128)(2,1)} %param.17), channel_id=1, replica_groups=mesh['seq'=8,'head'=4] {'seq'}, dimensions={1}, use_global_device_ids=true | all-gather | bytes 589824 | tf_op jit(solution)/shard_map/all_gather | solution.py:86
  86.1 5.1 collective-permute-start.1
  96.8 4.2 collective-permute-done.3
  101.0 6.9 collective-permute-done.4
  119.3 38.9 %all-reduce.5.cloned.1.call-done = f32[256,1024]{1,0:T(8,128)} async-done(((f32[256,1024]{1,0:T(8,128)}), f32[256,1024]{1,0:T(8,128)}) %all-reduce.5.cloned.1.call-update) | async-done | bytes 1048592 | tf_op jit(solution)/shard_map/psum | solution.py:119
  159.9 52.1 %all-gather.8.cloned.1.call-done = bf16[1024,1024]{1,0:T(8,128)(2,1)} async-done(((bf16[1024,128]{1,0:T(8,128)(2,1)}), bf16[1024,1024]{1,0:T(8,128)(2,1)}) %all-gather.8.cloned.1.call-update) | async-done | bytes 2097168 | tf_op jit(solution)/shard_map/all_gather | solution.py:86
  215.2 46.4 %all-gather.6.cloned.1.call-done = bf16[1024,1024]{1,0:T(8,128)(2,1)} async-done(((bf16[128,1024]{1,0:T(8,128)(2,1)}), bf16[1024,1024]{1,0:T(8,128)(2,1)}) %all-gather.6.cloned.1.call-update) | async-done | bytes 2097168 | tf_op jit(solution)/shard_map/all_gather | solution.py:85
  261.6 3.5 convert_reduce_fusion.2
  271.2 31.2 %all-reduce.9.cloned.1.call-done = f32[256,1024]{1,0:T(8,128)} async-done(((f32[256,1024]{1,0:T(8,128)}), f32[256,1024]{1,0:T(8,128)}) %all-reduce.9.cloned.1.call-update) | async-done | bytes 1048592 | tf_op jit(solution)/shard_map/psum | solution.py:132
  304.2 34.6 %all-reduce.7.cloned.1.call-done = bf16[256,1024]{1,0:T(8,128)(2,1)} async-done(((bf16[256,1024]{1,0:T(8,128)(2,1)}), bf16[256,1024]{1,0:T(8,128)(2,1)}) %all-reduce.7.cloned.1.call-update) | async-done | bytes 524304 | tf_op jit(solution)/shard_map/psum | solution.py:125
  363.6 4.2 collective-permute-start.10
  367.8 4.3 collective-permute-start.11
  379.3 4.2 collective-permute-start.9
  384.4 11.5 %collective-permute-done.11 = f32[2,256,256]{2,1,0:T(8,128)} collective-permute-done((f32[2,256,256]{2,1,0:T(8,128)}, f32[2,256,256]{2,1,0:T(8,128)}, u32[]{:S(2)}, u32[]{:S(2)}) %collective-permute-start.11) | collective-permute-done | bytes 524320 | tf_op jit(solution)/shard_map/ppermute | solution.py:19
  395.9 5.4 collective-permute-done.7
  401.3 10.7 %collective-permute-done.9 = f32[2,256,256]{2,1,0:T(8,128)} collective-permute-done((f32[2,256,256]{2,1,0:T(8,128)}, f32[2,256,256]{2,1,0:T(8,128)}, u32[]{:S(2)}, u32[]{:S(2)}) %collective-permute-start.9) | collective-permute-done | bytes 524320 | tf_op jit(solution)/shard_map/ppermute | solution.py:19
  415.9 41.7 %all-reduce.11.cloned.1.call-done = f32[256,1024]{1,0:T(8,128)} async-done(((f32[256,1024]{1,0:T(8,128)}), f32[256,1024]{1,0:T(8,128)}) %all-reduce.11.cloned.1.call-update) | async-done | bytes 1048592 | tf_op jit(solution)/shard_map/psum | solution.py:153
  472.1 22.1 %psum.39 = f32[1024]{0:T(1024)} all-reduce(f32[1024]{0:T(1024)S(1)} %get-tuple-element.20), channel_id=1, replica_groups=mesh['seq'=8,'head'=4] {'seq'}, use_global_device_ids=true, to_apply=%region_25.26 | all-reduce | flops 1024 | bytes 8192 | tf_op jit(solution)/shard_map/psum | solution.py:131
  495.5 19.4 %reduce-scatter.10.cloned.1.call-done = f32[5,128]{1,0:T(8,128)} async-done(((f32[5,1024]{1,0:T(8,128)}), f32[5,128]{1,0:T(8,128)}) %reduce-scatter.10.cloned.1.call-update) | async-done | bytes 2576 | tf_op jit(solution)/shard_map/reduce_scatter | solution.py:167
  516.3 65.9 %reduce-scatter.8.cloned.1.call-done = f32[256,128]{1,0:T(8,128)} async-done(((f32[256,1024]{1,0:T(8,128)}), f32[256,128]{1,0:T(8,128)}) %reduce-scatter.8.cloned.1.call-update) | async-done | bytes 131088 | tf_op jit(solution)/shard_map/reduce_scatter | solution.py:167
  582.2 78.2 %reduce-scatter.6.cloned.1.call-done = f32[128,3,256]{2,0,1:T(8,128)} async-done(((f32[1024,3,256]{2,0,1:T(8,128)}), f32[128,3,256]{2,0,1:T(8,128)}) %reduce-scatter.6.cloned.1.call-update) | async-done | bytes 393232 | tf_op jit(solution)/shard_map/reduce_scatter | solution.py:167
  660.4 91.4 %reduce-scatter.12.cloned.1.call-done = f32[128,1024]{1,0:T(8,128)} async-done(((f32[1024,1024]{1,0:T(8,128)}), f32[128,1024]{1,0:T(8,128)}) %reduce-scatter.12.cloned.1.call-update) | async-done | bytes 524304 | tf_op jit(solution)/shard_map/reduce_scatter | solution.py:167
  751.8 92.8 %reduce-scatter.14.cloned.1.call-done = f32[1024,128]{1,0:T(8,128)} async-done(((f32[1024,1024]{1,0:T(8,128)}), f32[1024,128]{1,0:T(8,128)}) %reduce-scatter.14.cloned.1.call-update) | async-done | bytes 524304 | tf_op jit(solution)/shard_map/reduce_scatter | solution.py:167
  (164 shorter events, 96.5 us)
Async XLA Ops:
  7.2 74.8 %all-gather.4.cloned.1.call-start = ((), (), s32[]{:S(2)}) async-start(), calls=%async_computation.5 | async-start | bytes 1769472 | tf_op jit(solution)/shard_map/all_gather | solution.py:85
  9.0 149.2 %all-reduce.5.cloned.1.call-start = ((), (), s32[]{:S(2)}) async-start(), calls=%async_computation.6 | async-start | bytes 2097152 | tf_op jit(solution)/shard_map/psum | solution.py:119
  84.2 11.1 %collective-permute-start = (bf16[2,256,256]{1,2,0:T(8,128)(2,1)S(1)}, bf16[2,256,256]{1,2,0:T(8,128)(2,1)S(1)}, u32[]{:S(2)}, u32[]{:S(2)}) collective-permute-start(bf16[2,256,256]{1,2,0:T(8,128)(2,1)S(1)} %pad_maximum_fusion.1), channel_id=1, source_target_pairs={{0,12},{4,16},{8,20},{12,24},{16,28},{1,13},{5,17},{9,21},{13,25},... | collective-permute-start | bytes 786440 | tf_op jit(solution)/shard_map/ppermute | solution.py:19
  86.1 10.6 %collective-permute-start.1 = (bf16[2,256,256]{1,2,0:T(8,128)(2,1)S(1)}, bf16[2,256,256]{1,2,0:T(8,128)(2,1)S(1)}, u32[]{:S(2)}, u32[]{:S(2)}) collective-permute-start(bf16[2,256,256]{1,2,0:T(8,128)(2,1)S(1)} %pad_maximum_fusion.1), channel_id=1, source_target_pairs={{0,8},{4,12},{8,16},{12,20},{16,24},{20,28},{1,9},{5,13},{9,17},{1... | collective-permute-start | bytes 786440 | tf_op jit(solution)/shard_map/ppermute | solution.py:19
  91.3 5.4 collective-permute-start.2
  92.7 8.3 collective-permute-start.3
  94.0 13.9 %collective-permute-start.4 = (bf16[2,256,256]{1,2,0:T(8,128)(2,1)S(1)}, bf16[2,256,256]{1,2,0:T(8,128)(2,1)S(1)}, u32[]{:S(2)}, u32[]{:S(2)}) collective-permute-start(bf16[2,256,256]{1,2,0:T(8,128)(2,1)S(1)} %pad_maximum_fusion.1), channel_id=1, source_target_pairs={{8,0},{12,4},{16,8},{20,12},{24,16},{28,20},{9,1},{13,5},{17,9},{2... | collective-permute-start | bytes 786440 | tf_op jit(solution)/shard_map/ppermute | solution.py:19
  95.3 12.6 %collective-permute-start.5 = (bf16[2,256,256]{1,2,0:T(8,128)(2,1)S(1)}, bf16[2,256,256]{1,2,0:T(8,128)(2,1)S(1)}, u32[]{:S(2)}, u32[]{:S(2)}) collective-permute-start(bf16[2,256,256]{1,2,0:T(8,128)(2,1)S(1)} %pad_maximum_fusion.1), channel_id=1, source_target_pairs={{12,0},{16,4},{20,8},{24,12},{28,16},{13,1},{17,5},{21,9},{25,13},... | collective-permute-start | bytes 786440 | tf_op jit(solution)/shard_map/ppermute | solution.py:19
  117.9 94.0 %all-gather.8.cloned.1.call-start = ((), (), s32[]{:S(2)}) async-start(), calls=%async_computation.8 | async-start | bytes 2359296 | tf_op jit(solution)/shard_map/all_gather | solution.py:86
  118.6 143.0 %all-gather.6.cloned.1.call-start = ((), (), s32[]{:S(2)}) async-start(), calls=%async_computation.7 | async-start | bytes 2359296 | tf_op jit(solution)/shard_map/all_gather | solution.py:85
  119.2 183.2 %all-reduce.9.cloned.1.call-start = ((), (), s32[]{:S(2)}) async-start(), calls=%async_computation.10 | async-start | bytes 2097152 | tf_op jit(solution)/shard_map/psum | solution.py:132
  267.7 71.1 %all-reduce.7.cloned.1.call-start = ((), (), s32[]{:S(2)}) async-start(), calls=%async_computation.9 | async-start | bytes 1048576 | tf_op jit(solution)/shard_map/psum | solution.py:125
  271.0 186.6 %all-reduce.11.cloned.1.call-start = ((), (), s32[]{:S(2)}) async-start(), calls=%async_computation.11 | async-start | bytes 2097152 | tf_op jit(solution)/shard_map/psum | solution.py:153
  363.6 15.7 %collective-permute-start.10 = (f32[2,256,256]{2,1,0:T(8,128)S(1)}, f32[2,256,256]{2,1,0:T(8,128)}, u32[]{:S(2)}, u32[]{:S(2)}) collective-permute-start(f32[2,256,256]{2,1,0:T(8,128)S(1)} %get-tuple-element.26), channel_id=1, source_target_pairs={{0,8},{4,12},{8,16},{12,20},{16,24},{20,28},{1,9},{5,13},{9,17},{1... | collective-permute-start | bytes 1572872 | tf_op jit(solution)/shard_map/ppermute | solution.py:19
  367.8 28.1 %collective-permute-start.11 = (f32[2,256,256]{2,1,0:T(8,128)}, f32[2,256,256]{2,1,0:T(8,128)}, u32[]{:S(2)}, u32[]{:S(2)}) collective-permute-start(f32[2,256,256]{2,1,0:T(8,128)} %get-tuple-element.25), channel_id=1, source_target_pairs={{0,12},{4,16},{8,20},{12,24},{16,28},{1,13},{5,17},{9,21},{13,25},... | collective-permute-start | bytes 1572872 | tf_op jit(solution)/shard_map/ppermute | solution.py:19
  372.1 23.9 %collective-permute-start.6 = (f32[2,256,256]{2,1,0:T(8,128)}, f32[2,256,256]{2,1,0:T(8,128)}, u32[]{:S(2)}, u32[]{:S(2)}) collective-permute-start(f32[2,256,256]{2,1,0:T(8,128)} %get-tuple-element.24), channel_id=1, source_target_pairs={{12,0},{16,4},{20,8},{24,12},{28,16},{13,1},{17,5},{21,9},{25,13},... | collective-permute-start | bytes 1572872 | tf_op jit(solution)/shard_map/ppermute | solution.py:19
  373.3 28.0 %collective-permute-start.7 = (f32[2,256,256]{2,1,0:T(8,128)}, f32[2,256,256]{2,1,0:T(8,128)}, u32[]{:S(2)}, u32[]{:S(2)}) collective-permute-start(f32[2,256,256]{2,1,0:T(8,128)} %get-tuple-element.29), channel_id=1, source_target_pairs={{8,0},{12,4},{16,8},{20,12},{24,16},{28,20},{9,1},{13,5},{17,9},{2... | collective-permute-start | bytes 1572872 | tf_op jit(solution)/shard_map/ppermute | solution.py:19
  374.6 26.7 %collective-permute-start.8 = (f32[2,256,256]{2,1,0:T(8,128)}, f32[2,256,256]{2,1,0:T(8,128)}, u32[]{:S(2)}, u32[]{:S(2)}) collective-permute-start(f32[2,256,256]{2,1,0:T(8,128)} %get-tuple-element.28), channel_id=1, source_target_pairs={{4,0},{8,4},{12,8},{16,12},{20,16},{24,20},{28,24},{5,1},{9,5},{13... | collective-permute-start | bytes 1572872 | tf_op jit(solution)/shard_map/ppermute | solution.py:19
  379.3 32.7 %collective-permute-start.9 = (f32[2,256,256]{2,1,0:T(8,128)}, f32[2,256,256]{2,1,0:T(8,128)}, u32[]{:S(2)}, u32[]{:S(2)}) collective-permute-start(f32[2,256,256]{2,1,0:T(8,128)} %get-tuple-element.27), channel_id=1, source_target_pairs={{0,4},{4,8},{8,12},{12,16},{16,20},{20,24},{24,28},{1,5},{5,9},{9,... | collective-permute-start | bytes 1572872 | tf_op jit(solution)/shard_map/ppermute | solution.py:19
  415.9 99.1 %reduce-scatter.10.cloned.1.call-start = ((), (), s32[]{:S(2)}) async-start(), calls=%async_computation.14 | async-start | bytes 36864 | tf_op jit(solution)/shard_map/reduce_scatter | solution.py:167
  460.0 122.2 %reduce-scatter.8.cloned.1.call-start = ((), (), s32[]{:S(2)}) async-start(), calls=%async_computation.13 | async-start | bytes 1179648 | tf_op jit(solution)/shard_map/reduce_scatter | solution.py:167
  461.4 199.0 %reduce-scatter.6.cloned.1.call-start = ((), (), s32[]{:S(2)}) async-start(), calls=%async_computation.12 | async-start | bytes 3538944 | tf_op jit(solution)/shard_map/reduce_scatter | solution.py:167
  464.0 287.9 %reduce-scatter.12.cloned.1.call-start = ((), (), s32[]{:S(2)}) async-start(), calls=%async_computation.15 | async-start | bytes 4718592 | tf_op jit(solution)/shard_map/reduce_scatter | solution.py:167
  467.8 376.8 %reduce-scatter.14.cloned.1.call-start = ((), (), s32[]{:S(2)}) async-start(), calls=%async_computation.16 | async-start | bytes 4718592 | tf_op jit(solution)/shard_map/reduce_scatter | solution.py:167
  (21 other events, 298.2 us)
Sparse Core Ops, SparseCore 0:
  10.6 48.0 all-gather.3
  118.0 40.1 all-reduce.4
  160.5 51.4 all-gather.7
  214.1 47.4 all-gather.5
  267.8 34.5 all-reduce.8
  305.2 33.5 all-reduce.6
  416.0 41.5 all-reduce.10
  461.0 53.8 reduce-scatter.9
  519.3 62.8 reduce-scatter.7
  586.3 74.0 reduce-scatter.5
  664.6 87.1 reduce-scatter.11
  756.3 88.2 reduce-scatter.13
where the time goes:
time: 853 us; the launch traced here: 851 us
  waiting for transfers between devices  636 us (75%)
  blocking collectives  77.8 us (9%)
  matrix products  35.6 us (4%)
  starting transfers between devices  29.3 us (3%)
  local copies, waits for them, and re-layouts  29.2 us (3%)
  between operations  24.6 us (3%)
  other arithmetic  18.9 us (2%)
    reduce_scatter x5, waiting for transfers between devices, local_general(): lax.psum_scatter(v, 'seq', scatter_dimension=d, tiled=True)  348 us
    all_gather x2, blocking collectives, local_general(): cols = lambda v: lax.all_gather(v, 'seq', axis=1, tiled=True)  55.7 us
    all_gather x1, waiting for transfers between devices, local_general(): cols = lambda v: lax.all_gather(v, 'seq', axis=1, tiled=True)  52.1 us
    all_gather x2, waiting for transfers between devices, local_general(): rows = lambda v: lax.all_gather(v, 'seq', axis=0, tiled=True)  46.4 us
    ppermute x12, waiting for transfers between devices, shifted(): lax.ppermute(value, axis, [(i, i + steps) for i in range(first, last)])  42.2 us
    psum x1, waiting for transfers between devices, local_general(): lax.psum(jnp.einsum('tcf,dcf->td', grad_triple, qkv, preferred_element_ty...  41.7 us
    psum x1, waiting for transfers between devices, local_general(): middle = inputs + lax.psum(dot(attended, out_w, ((1,), (0,))), 'head')  38.9 us
    psum x1, waiting for transfers between devices, local_general(): lax.psum(dot(hidden, down_w, ((1,), (0,))).astype(BF16), 'head').astype(F32)  34.6 us
  transfers between devices with their start and end apart: 24, of which 17 were waited for; matrix products, arithmetic and copies ran while one was open for 4% of the time, Pallas kernels for 0%

commit v1 on v0

--- a/solution.py
+++ b/solution.py
@@ -11,6 +11,18 @@
 NEGATIVE = -1e30
 F32 = jnp.float32
 BF16 = jnp.bfloat16
+
+
+def doubled_up(x, axis, dim):
+    ways, here = (lax.axis_size(axis), lax.axis_index(axis))
+    grown, reach = (x, 1)
+    while reach < ways:
+        theirs = lax.ppermute(grown, axis, [(d, d ^ reach) for d in range(ways)])
+        mine_first = jnp.concatenate([grown, theirs], axis=dim)
+        theirs_first = jnp.concatenate([theirs, grown], axis=dim)
+        grown = jnp.where(here & reach == 0, mine_first, theirs_first)
+        reach = 2 * reach
+    return grown
 
 
 def shifted(value, axis, steps):
@@ -83,7 +95,7 @@
     tok, width = tokens.shape
     heads = w_qkv.shape[2] // HEAD_DIM
     rows = lambda v: lax.all_gather(v, "seq", axis=0, tiled=True)
-    cols = lambda v: lax.all_gather(v, "seq", axis=1, tiled=True)
+    cols = lambda v: doubled_up(v, "seq", 1)
     vectors = jnp.stack([ln1_gain, ln1_bias, ln2_gain, ln2_bias, down_bias], axis=0)
     gain_one, shift_one, gain_two, shift_two, down_shift = [
         v[None].astype(F32) for v in cols(vectors)

time: 853 us -> 818 us (0.959)
  blocking collectives: 77.8 us -> 21.9 us
  starting transfers between devices: 29.3 us -> 50.3 us
  waiting for transfers between devices: 636 us -> 627 us
    all_gather x2 -> x0, blocking collectives: 55.7 us -> none  [local_general(): cols = lambda v: lax.all_gather(v, 'seq', axis=1, tiled=True)]
    all_gather x1 -> x0, waiting for transfers between devices: 52.1 us -> none  [local_general(): cols = lambda v: lax.all_gather(v, 'seq', axis=1, tiled=True)]
    all_gather x2, waiting for transfers between devices: 46.4 us -> 88.3 us  [local_general(): rows = lambda v: lax.all_gather(v, 'seq', axis=0, tiled=True)]
    psum x1, waiting for transfers between devices: 38.9 us -> 11.6 us  [local_general(): middle = inputs + lax.psum(dot(attended, out_w, ((1,), (0,))), 'head')]
    ppermute x0 -> x9, waiting for transfers between devices: none -> 20.6 us  [doubled_up(): theirs = lax.ppermute(grown, axis, [(d, d ^ reach) for d in range(ways)])]
    ppermute x0 -> x9, starting transfers between devices: none -> 16.6 us  [doubled_up(): theirs = lax.ppermute(grown, axis, [(d, d ^ reach) for d in range(ways)])]
    psum x1, waiting for transfers between devices: 41.7 us -> 56 us  [local_general(): lax.psum(jnp.einsum('tcf,dcf->td', grad_triple, qkv, preferred_element_ty...]
  transfers between devices with their start and end apart: 24 -> 32, of which waited for: 17 -> 22; matrix products, arithmetic and copies ran while one was open for 4% -> 6% of each run, Pallas kernels for 0% -> 0%
where the time goes in v1:
time: 818 us; the launch traced here: 817 us
  waiting for transfers between devices  627 us (77%)
  starting transfers between devices  50.3 us (6%)
  matrix products  40.5 us (5%)
  local copies, waits for them, and re-layouts  28.5 us (3%)
  between operations  24.4 us (3%)
  other arithmetic  23.6 us (3%)
  blocking collectives  21.9 us (3%)
    reduce_scatter x5, waiting for transfers between devices, local_general(): lax.psum_scatter(v, 'seq', scatter_dimension=d, tiled=True)  346 us
    all_gather x2, waiting for transfers between devices, local_general(): rows = lambda v: lax.all_gather(v, 'seq', axis=0, tiled=True)  88.3 us
    psum x1, waiting for transfers between devices, local_general(): lax.psum(jnp.einsum('tcf,dcf->td', grad_triple, qkv, preferred_element_ty...  56 us
    ppermute x12, waiting for transfers between devices, shifted(): lax.ppermute(value, axis, [(i, i + steps) for i in range(first, last)])  41 us
    ppermute x12, starting transfers between devices, shifted(): lax.ppermute(value, axis, [(i, i + steps) for i in range(first, last)])  33 us
    psum x1, waiting for transfers between devices, local_general(): lax.psum(dot(hidden, down_w, ((1,), (0,))).astype(BF16), 'head').astype(F32)  32.9 us
    psum x1, waiting for transfers between devices, local_general(): grad_two = lax.psum(dot(grad_pre, up_w, ((1,), (1,))), 'head')  30 us
    dot_general x9, matrix products, dot(): return lax.dot_general(a, b, (dims, ((), ())), preferred_element_type=F32)  25.3 us
  transfers between devices with their start and end apart: 32, of which 22 were waited for; matrix products, arithmetic and copies ran while one was open for 6% of the time, Pallas kernels for 0%

profile of v1, /device:TPU:0, one launch (start us, length us, event | category | flops | bytes accessed | tf_op | source)
XLA Modules:
  0.0 816.7 jit_solution(5098405033179958429)
XLA Ops:
  37.2 21.7 %all-gather.3.cloned.1.call-done = bf16[1024,3,256]{0,2,1:T(8,128)(2,1)} async-done(((bf16[128,3,256]{0,2,1:T(8,128)(2,1)}), bf16[1024,3,256]{0,2,1:T(8,128)(2,1)}) %all-gather.3.cloned.1.call-update) | async-done | bytes 1572880 | tf_op jit(solution)/shard_map/all_gather | solution.py:97
  79.9 10.6 %collective-permute-done.7 = bf16[2,256,256]{1,2,0:T(8,128)(2,1)S(1)} collective-permute-done((bf16[2,256,256]{1,2,0:T(8,128)(2,1)S(1)}, bf16[2,256,256]{1,2,0:T(8,128)(2,1)S(1)}, u32[]{:S(2)}, u32[]{:S(2)}) %collective-permute-start.7) | collective-permute-done | bytes 262176 | tf_op jit(solution)/shard_map/ppermute | solution.py:31
  90.5 6.0 collective-permute-done.8
  108.4 8.3 %collective-permute-start.12 = (bf16[1024,128]{1,0:T(8,128)(2,1)S(1)}, bf16[1024,128]{1,0:T(8,128)(2,1)S(1)}, u32[]{:S(2)}, u32[]{:S(2)}) collective-permute-start(bf16[1024,128]{1,0:T(8,128)(2,1)S(1)} %copy-done.17), channel_id=1, source_target_pairs={{0,4},{4,0},{8,12},{12,8},{16,20},{20,16},{24,28},{28,24},{1,5},{5... | collective-permute-start | bytes 786440 | tf_op jit(solution)/shard_map/ppermute | solution.py:20
  116.7 6.0 collective-permute-done.12
  123.0 12.8 %collective-permute-done.13 = bf16[1024,256]{1,0:T(8,128)(2,1)S(1)} collective-permute-done((bf16[1024,256]{1,0:T(8,128)(2,1)S(1)}, bf16[1024,256]{1,0:T(8,128)(2,1)S(1)}, u32[]{:S(2)}, u32[]{:S(2)}) %collective-permute-start.13) | collective-permute-done | bytes 524320 | tf_op jit(solution)/shard_map/ppermute | solution.py:20
  137.2 11.6 %all-reduce.5.cloned.1.call-done = f32[256,1024]{1,0:T(8,128)} async-done(((f32[256,1024]{1,0:T(8,128)}), f32[256,1024]{1,0:T(8,128)}) %all-reduce.5.cloned.1.call-update) | async-done | bytes 1048592 | tf_op jit(solution)/shard_map/psum | solution.py:131
  150.5 66.6 %all-gather.5.cloned.1.call-done = bf16[1024,1024]{1,0:T(8,128)(2,1)} async-done(((bf16[128,1024]{1,0:T(8,128)(2,1)}), bf16[1024,1024]{1,0:T(8,128)(2,1)}) %all-gather.5.cloned.1.call-update) | async-done | bytes 2097168 | tf_op jit(solution)/shard_map/all_gather | solution.py:97
  219.5 4.6 convert_reduce_fusion.2
  226.1 4.5 convolution_convert_fusion
  230.7 30.0 %all-reduce.9.cloned.1.call-done = f32[256,1024]{1,0:T(8,128)} async-done(((f32[256,1024]{1,0:T(8,128)}), f32[256,1024]{1,0:T(8,128)}) %all-reduce.9.cloned.1.call-update) | async-done | bytes 1048592 | tf_op jit(solution)/shard_map/psum | solution.py:144
  264.1 32.9 %all-reduce.7.cloned.1.call-done = bf16[256,1024]{1,0:T(8,128)(2,1)} async-done(((bf16[256,1024]{1,0:T(8,128)(2,1)}), bf16[256,1024]{1,0:T(8,128)(2,1)}) %all-reduce.7.cloned.1.call-update) | async-done | bytes 524304 | tf_op jit(solution)/shard_map/psum | solution.py:137
  327.2 5.4 collective-permute-start.18
  332.5 4.7 collective-permute-start.19
  341.1 6.0 collective-permute-start.20
  351.5 11.7 %collective-permute-done.18 = f32[2,256,256]{2,1,0:T(8,128)} collective-permute-done((f32[2,256,256]{2,1,0:T(8,128)}, f32[2,256,256]{2,1,0:T(8,128)}, u32[]{:S(2)}, u32[]{:S(2)}) %collective-permute-start.18) | collective-permute-done | bytes 524320 | tf_op jit(solution)/shard_map/ppermute | solution.py:31
  367.1 56.0 %all-reduce.11.cloned.1.call-done = f32[256,1024]{1,0:T(8,128)} async-done(((f32[256,1024]{1,0:T(8,128)}), f32[256,1024]{1,0:T(8,128)}) %all-reduce.11.cloned.1.call-update) | async-done | bytes 1048592 | tf_op jit(solution)/shard_map/psum | solution.py:165
  434.3 4.1 fusion.47
  439.2 21.9 %psum.39 = f32[1024]{0:T(1024)} all-reduce(f32[1024]{0:T(1024)S(1)} %copy-done.35), channel_id=1, replica_groups=mesh['seq'=8,'head'=4] {'seq'}, use_global_device_ids=true, to_apply=%region_25.26 | all-reduce | flops 1024 | bytes 8192 | tf_op jit(solution)/shard_map/psum | solution.py:143
  462.5 18.0 %reduce-scatter.10.cloned.1.call-done = f32[5,128]{1,0:T(8,128)} async-done(((f32[5,1024]{1,0:T(8,128)}), f32[5,128]{1,0:T(8,128)}) %reduce-scatter.10.cloned.1.call-update) | async-done | bytes 2576 | tf_op jit(solution)/shard_map/reduce_scatter | solution.py:179
  481.8 65.9 %reduce-scatter.8.cloned.1.call-done = f32[256,128]{1,0:T(8,128)} async-done(((f32[256,1024]{1,0:T(8,128)}), f32[256,128]{1,0:T(8,128)}) %reduce-scatter.8.cloned.1.call-update) | async-done | bytes 131088 | tf_op jit(solution)/shard_map/reduce_scatter | solution.py:179
  547.8 78.3 %reduce-scatter.6.cloned.1.call-done = f32[128,3,256]{2,0,1:T(8,128)} async-done(((f32[1024,3,256]{2,0,1:T(8,128)}), f32[128,3,256]{2,0,1:T(8,128)}) %reduce-scatter.6.cloned.1.call-update) | async-done | bytes 393232 | tf_op jit(solution)/shard_map/reduce_scatter | solution.py:179
  626.1 91.1 %reduce-scatter.12.cloned.1.call-done = f32[128,1024]{1,0:T(8,128)} async-done(((f32[1024,1024]{1,0:T(8,128)}), f32[128,1024]{1,0:T(8,128)}) %reduce-scatter.12.cloned.1.call-update) | async-done | bytes 524304 | tf_op jit(solution)/shard_map/reduce_scatter | solution.py:179
  717.2 92.9 %reduce-scatter.14.cloned.1.call-done = f32[1024,128]{1,0:T(8,128)} async-done(((f32[1024,1024]{1,0:T(8,128)}), f32[1024,128]{1,0:T(8,128)}) %reduce-scatter.14.cloned.1.call-update) | async-done | bytes 524304 | tf_op jit(solution)/shard_map/reduce_scatter | solution.py:179
  (216 shorter events, 120.5 us)
Async XLA Ops:
  7.2 51.7 %all-gather.3.cloned.1.call-start = ((), (), s32[]{:S(2)}) async-start(), calls=%async_computation.5 | async-start | bytes 1769472 | tf_op jit(solution)/shard_map/all_gather | solution.py:97
  8.0 17.4 %collective-permute-start = (bf16[5,128]{1,0:T(8,128)(2,1)S(1)}, bf16[5,128]{1,0:T(8,128)(2,1)S(1)}, u32[]{:S(2)}, u32[]{:S(2)}) collective-permute-start(bf16[5,128]{1,0:T(8,128)(2,1)S(1)} %stack.75), channel_id=1, source_target_pairs={{0,4},{4,0},{8,12},{12,8},{16,20},{20,16},{24,28},{28,24},{1,5},{5... | collective-permute-start | bytes 3848 | tf_op jit(solution)/shard_map/ppermute | solution.py:20
  12.8 136.0 %all-reduce.5.cloned.1.call-start = ((), (), s32[]{:S(2)}) async-start(), calls=%async_computation.6 | async-start | bytes 2097152 | tf_op jit(solution)/shard_map/psum | solution.py:131
  12.9 23.9 %collective-permute-start.9 = (bf16[256,128]{1,0:T(8,128)(2,1)}, bf16[256,128]{1,0:T(8,128)(2,1)S(1)}, u32[]{:S(2)}, u32[]{:S(2)}) collective-permute-start(bf16[256,128]{1,0:T(8,128)(2,1)} %param.17), channel_id=1, source_target_pairs={{0,4},{4,0},{8,12},{12,8},{16,20},{20,16},{24,28},{28,24},{1,5},{5... | collective-permute-start | bytes 196616 | tf_op jit(solution)/shard_map/ppermute | solution.py:20
  36.9 30.2 %collective-permute-start.10 = (bf16[256,256]{1,0:T(8,128)(2,1)S(1)}, bf16[256,256]{1,0:T(8,128)(2,1)S(1)}, u32[]{:S(2)}, u32[]{:S(2)}) collective-permute-start(bf16[256,256]{1,0:T(8,128)(2,1)S(1)} %maximum_select_fusion.7), channel_id=1, source_target_pairs={{0,8},{4,12},{8,0},{12,4},{16,24},{20,28},{24,16},{28,20},{1,9},{5... | collective-permute-start | bytes 393224 | tf_op jit(solution)/shard_map/ppermute | solution.py:20
  67.2 37.9 %collective-permute-start.11 = (bf16[256,512]{1,0:T(8,128)(2,1)S(1)}, bf16[256,512]{1,0:T(8,128)(2,1)}, u32[]{:S(2)}, u32[]{:S(2)}) collective-permute-start(bf16[256,512]{1,0:T(8,128)(2,1)S(1)} %maximum_select_fusion.6), channel_id=1, source_target_pairs={{0,16},{4,20},{8,24},{12,28},{16,0},{20,4},{24,8},{28,12},{1,17},{... | collective-permute-start | bytes 786440 | tf_op jit(solution)/shard_map/ppermute | solution.py:20
  72.0 18.6 %collective-permute-start.7 = (bf16[2,256,256]{1,2,0:T(8,128)(2,1)S(1)}, bf16[2,256,256]{1,2,0:T(8,128)(2,1)S(1)}, u32[]{:S(2)}, u32[]{:S(2)}) collective-permute-start(bf16[2,256,256]{1,2,0:T(8,128)(2,1)S(1)} %pad_maximum_fusion.1), channel_id=1, source_target_pairs={{8,0},{12,4},{16,8},{20,12},{24,16},{28,20},{9,1},{13,5},{17,9},{2... | collective-permute-start | bytes 786440 | tf_op jit(solution)/shard_map/ppermute | solution.py:31
  75.1 21.5 %collective-permute-start.8 = (bf16[2,256,256]{1,2,0:T(8,128)(2,1)S(1)}, bf16[2,256,256]{1,2,0:T(8,128)(2,1)S(1)}, u32[]{:S(2)}, u32[]{:S(2)}) collective-permute-start(bf16[2,256,256]{1,2,0:T(8,128)(2,1)S(1)} %pad_maximum_fusion.1), channel_id=1, source_target_pairs={{12,0},{16,4},{20,8},{24,12},{28,16},{13,1},{17,5},{21,9},{25,13},... | collective-permute-start | bytes 786440 | tf_op jit(solution)/shard_map/ppermute | solution.py:31
  107.6 109.4 %all-gather.5.cloned.1.call-start = ((), (), s32[]{:S(2)}) async-start(), calls=%async_computation.7 | async-start | bytes 2359296 | tf_op jit(solution)/shard_map/all_gather | solution.py:97
  108.3 152.3 %all-reduce.9.cloned.1.call-start = ((), (), s32[]{:S(2)}) async-start(), calls=%async_computation.9 | async-start | bytes 2097152 | tf_op jit(solution)/shard_map/psum | solution.py:144
  137.2 82.3 %collective-permute-start.14 = (bf16[1024,512]{1,0:T(8,128)(2,1)}, bf16[1024,512]{1,0:T(8,128)(2,1)}, u32[]{:S(2)}, u32[]{:S(2)}) collective-permute-start(bf16[1024,512]{1,0:T(8,128)(2,1)} %maximum_select_fusion.1), channel_id=1, source_target_pairs={{0,16},{4,20},{8,24},{12,28},{16,0},{20,4},{24,8},{28,12},{1,17},{... | collective-permute-start | bytes 3145736 | tf_op jit(solution)/shard_map/ppermute | solution.py:20
  225.9 71.1 %all-reduce.7.cloned.1.call-start = ((), (), s32[]{:S(2)}) async-start(), calls=%async_computation.8 | async-start | bytes 1048576 | tf_op jit(solution)/shard_map/psum | solution.py:137
  230.6 192.5 %all-reduce.11.cloned.1.call-start = ((), (), s32[]{:S(2)}) async-start(), calls=%async_computation.10 | async-start | bytes 2097152 | tf_op jit(solution)/shard_map/psum | solution.py:165
  323.3 17.8 %collective-permute-start.15 = (f32[2,256,256]{2,1,0:T(8,128)S(1)}, f32[2,256,256]{2,1,0:T(8,128)}, u32[]{:S(2)}, u32[]{:S(2)}) collective-permute-start(f32[2,256,256]{2,1,0:T(8,128)S(1)} %get-tuple-element.22), channel_id=1, source_target_pairs={{12,0},{16,4},{20,8},{24,12},{28,16},{13,1},{17,5},{21,9},{25,13},... | collective-permute-start | bytes 1572872 | tf_op jit(solution)/shard_map/ppermute | solution.py:31
  324.6 26.9 %collective-permute-start.16 = (f32[2,256,256]{2,1,0:T(8,128)}, f32[2,256,256]{2,1,0:T(8,128)}, u32[]{:S(2)}, u32[]{:S(2)}) collective-permute-start(f32[2,256,256]{2,1,0:T(8,128)} %get-tuple-element.27), channel_id=1, source_target_pairs={{8,0},{12,4},{16,8},{20,12},{24,16},{28,20},{9,1},{13,5},{17,9},{2... | collective-permute-start | bytes 1572872 | tf_op jit(solution)/shard_map/ppermute | solution.py:31
  325.9 25.6 %collective-permute-start.17 = (f32[2,256,256]{2,1,0:T(8,128)}, f32[2,256,256]{2,1,0:T(8,128)}, u32[]{:S(2)}, u32[]{:S(2)}) collective-permute-start(f32[2,256,256]{2,1,0:T(8,128)} %get-tuple-element.26), channel_id=1, source_target_pairs={{4,0},{8,4},{12,8},{16,12},{20,16},{24,20},{28,24},{5,1},{9,5},{13... | collective-permute-start | bytes 1572872 | tf_op jit(solution)/shard_map/ppermute | solution.py:31
  327.2 36.0 %collective-permute-start.18 = (f32[2,256,256]{2,1,0:T(8,128)}, f32[2,256,256]{2,1,0:T(8,128)}, u32[]{:S(2)}, u32[]{:S(2)}) collective-permute-start(f32[2,256,256]{2,1,0:T(8,128)} %get-tuple-element.25), channel_id=1, source_target_pairs={{0,4},{4,8},{8,12},{12,16},{16,20},{20,24},{24,28},{1,5},{5,9},{9,... | collective-permute-start | bytes 1572872 | tf_op jit(solution)/shard_map/ppermute | solution.py:31
  332.5 30.7 %collective-permute-start.19 = (f32[2,256,256]{2,1,0:T(8,128)}, f32[2,256,256]{2,1,0:T(8,128)}, u32[]{:S(2)}, u32[]{:S(2)}) collective-permute-start(f32[2,256,256]{2,1,0:T(8,128)} %get-tuple-element.24), channel_id=1, source_target_pairs={{0,8},{4,12},{8,16},{12,20},{16,24},{20,28},{1,9},{5,13},{9,17},{1... | collective-permute-start | bytes 1572872 | tf_op jit(solution)/shard_map/ppermute | solution.py:31
  341.1 22.1 %collective-permute-start.20 = (f32[2,256,256]{2,1,0:T(8,128)}, f32[2,256,256]{2,1,0:T(8,128)}, u32[]{:S(2)}, u32[]{:S(2)}) collective-permute-start(f32[2,256,256]{2,1,0:T(8,128)} %get-tuple-element.23), channel_id=1, source_target_pairs={{0,12},{4,16},{8,20},{12,24},{16,28},{1,13},{5,17},{9,21},{13,25},... | collective-permute-start | bytes 1572872 | tf_op jit(solution)/shard_map/ppermute | solution.py:31
  367.1 113.3 %reduce-scatter.10.cloned.1.call-start = ((), (), s32[]{:S(2)}) async-start(), calls=%async_computation.13 | async-start | bytes 36864 | tf_op jit(solution)/shard_map/reduce_scatter | solution.py:179
  425.6 122.2 %reduce-scatter.8.cloned.1.call-start = ((), (), s32[]{:S(2)}) async-start(), calls=%async_computation.12 | async-start | bytes 1179648 | tf_op jit(solution)/shard_map/reduce_scatter | solution.py:179
  426.9 199.2 %reduce-scatter.6.cloned.1.call-start = ((), (), s32[]{:S(2)}) async-start(), calls=%async_computation.11 | async-start | bytes 3538944 | tf_op jit(solution)/shard_map/reduce_scatter | solution.py:179
  429.5 287.8 %reduce-scatter.12.cloned.1.call-start = ((), (), s32[]{:S(2)}) async-start(), calls=%async_computation.14 | async-start | bytes 4718592 | tf_op jit(solution)/shard_map/reduce_scatter | solution.py:179
  433.3 376.8 %reduce-scatter.14.cloned.1.call-start = ((), (), s32[]{:S(2)}) async-start(), calls=%async_computation.15 | async-start | bytes 4718592 | tf_op jit(solution)/shard_map/reduce_scatter | solution.py:179
  (45 other events, 991.2 us)
Sparse Core Ops, SparseCore 0:
  13.0 45.9 all-gather.2
  107.7 41.0 all-reduce.4
  151.1 65.8 all-gather.4
  226.0 34.5 all-reduce.8
  263.4 33.5 all-reduce.6
  367.2 55.8 all-reduce.10
  426.5 53.8 reduce-scatter.9
  484.8 62.9 reduce-scatter.7
  551.9 74.0 reduce-scatter.5
  630.1 87.0 reduce-scatter.11
  721.9 88.2 reduce-scatter.13
